TPU v7x, 256 devices: a whole 4x4x8 slice. The times are simulated.
256 devices in a mesh: seq: 8 (over x, y_hi), dp: 32 (over y_lo, z, core).
Axes of the slice: x: 4, y: 4 (y_hi: 2, y_lo: 2; y = y_hi * 2 + y_lo), z: 8, core: 2. Of those that a mesh axis runs over, the one named last changes fastest.
Arguments:
- frames: bfloat16 [64, 1024, 3072], P('dp', 'seq'), may hold values from -6 to 6
- proj_weight: bfloat16 [3072, 4608], P('dp'), may hold values from -0.109375 to 0.109375
- rate_weight: bfloat16 [3072, 24], replicated, may hold values from -0.109375 to 0.109375
- rate_bias: float32 [24], replicated, may hold values from -2 to 1
- init_weights: float32 [2, 24, 64, 256], replicated, may hold values from -0.75 to 0.75
- init_bias_hidden: float32 [24, 256], replicated, may hold values from -3 to 3
- init_bias_out: float32 [24, 64], replicated, may hold values from -3 to 3
- out_gain: float32 [1536], replicated, may hold values from 0.5 to 1.5
Outputs:
- ttt_output: bfloat16 [64, 1024, 1536], P('dp', 'seq')
All inputs are finite; a program needn't handle non-finite values.
Results may differ from a plain program's by a relative error of at most 0.0091.
Values may be sent and summed in bfloat16 or wider, within the bound.
No kernel may reach another device: no remote copies, remote signals or barrier semaphores. Data moves between devices by JAX's collectives and lax.ppermute only.
A program may use at most 128 MiB of HBM per device.

v0:
```python
import math
import jax
import jax.numpy as jnp
from jax import lax
from jax.sharding import PartitionSpec as P

MB = 64
precise = lax.Precision.HIGHEST
coefficient = 0.044715
root_scale = math.sqrt(2.0 / math.pi)


def shortened(x):
    return jax.tree.map(lambda a: a.astype(jnp.bfloat16) if a.dtype == jnp.float32 else a, x)


def shifted(block, axis, distance):
    devices = range(lax.axis_size(axis))
    route = [(i - distance, i) for i in devices if i - distance in devices]
    return lax.ppermute(block, axis, route)


def gelu_pair(z_value):
    tanh_part = jnp.tanh(root_scale * (z_value + coefficient * z_value * z_value * z_value))
    result = 0.5 * z_value * (1.0 + tanh_part)
    derivative = 0.5 * (1.0 + tanh_part) + 0.5 * z_value * (
        1.0 - tanh_part * tanh_part
    ) * root_scale * (1.0 + 3.0 * coefficient * z_value * z_value)
    return (result, derivative)


def minibatch(carried, inputs):
    pair, bias_hidden, bias_out = carried
    queries, key_rows, values, step_rate = inputs
    w_first = pair[0]
    w_second = pair[1]
    block_len = queries.shape[1]
    causal = jnp.tril(jnp.ones((block_len, block_len), dtype=bool))
    z_first = (
        jnp.einsum("hbd,hdf->hbf", key_rows, w_first, precision=precise) + bias_hidden[:, None, :]
    )
    hidden, derivative = gelu_pair(z_first)
    z_second = (
        jnp.einsum("hbf,hdf->hbd", hidden, w_second, precision=precise) + bias_out[:, None, :]
    )
    grad_second = z_second - (values - key_rows)
    grad_first = jnp.einsum("hbd,hdf->hbf", grad_second, w_second, precision=precise) * derivative
    scores_first = jnp.einsum("htd,hsd->hts", queries, key_rows, precision=precise) + 1.0
    mix_first = jnp.where(causal[None], scores_first * step_rate[:, None, :], 0.0)
    zq_first = (
        jnp.einsum("htd,hdf->htf", queries, w_first, precision=precise) + bias_hidden[:, None, :]
    )
    zq_first = zq_first - jnp.einsum("hts,hsf->htf", mix_first, grad_first, precision=precise)
    hidden_query, unused = gelu_pair(zq_first)
    scores_second = jnp.einsum("htf,hsf->hts", hidden_query, hidden, precision=precise) + 1.0
    mix_second = jnp.where(causal[None], scores_second * step_rate[:, None, :], 0.0)
    zq_second = (
        jnp.einsum("htf,hdf->htd", hidden_query, w_second, precision=precise) + bias_out[:, None, :]
    )
    zq_second = zq_second - jnp.einsum("hts,hsd->htd", mix_second, grad_second, precision=precise)
    scaled_first = grad_first * step_rate[:, :, None]
    scaled_second = grad_second * step_rate[:, :, None]
    new_first = w_first - jnp.einsum("hbd,hbf->hdf", key_rows, scaled_first, precision=precise)
    new_second = w_second - jnp.einsum("hbd,hbf->hdf", scaled_second, hidden, precision=precise)
    new_pair = jnp.stack([new_first, new_second])
    new_hidden = bias_hidden - jnp.sum(scaled_first, axis=1)
    new_out = bias_out - jnp.sum(scaled_second, axis=1)
    return ((new_pair, new_hidden, new_out), queries + zq_second)


def run_slab(start_state, column_block, rate_block, gain_rows):
    slab_len = column_block.shape[0]
    group_heads = column_block.shape[2]
    head_size = column_block.shape[3]
    batches = slab_len // MB
    inputs = (
        column_block.astype(jnp.float32)
        .reshape(batches, MB, 3, group_heads, head_size)
        .transpose(2, 0, 3, 1, 4)
    )
    step_rate = rate_block.reshape(batches, MB, group_heads).transpose(0, 2, 1)
    final_state, results = lax.scan(
        minibatch, start_state, (inputs[0], inputs[1], inputs[2], step_rate)
    )
    results = results.transpose(0, 2, 1, 3).reshape(slab_len, group_heads, head_size)
    normed = (
        results * lax.rsqrt(jnp.mean(results * results, axis=-1, keepdims=True) + 1e-06) * gain_rows
    )
    return (final_state, normed.reshape(slab_len, group_heads * head_size).astype(jnp.bfloat16))


def on_device(
    frames,
    proj_weight,
    rate_weight,
    rate_bias,
    init_weights,
    init_bias_hidden,
    init_bias_out,
    out_gain,
):
    clip_count, slab_len, model_width = frames.shape
    head_count = rate_weight.shape[1]
    head_size = init_weights.shape[2]
    inner_width = init_weights.shape[3]
    token_rows = frames.reshape(clip_count * slab_len, model_width)
    full_weight = lax.all_gather(proj_weight, "dp", axis=0, tiled=True)
    projected = jnp.dot(token_rows, full_weight, preferred_element_type=jnp.float32)
    projected = projected.astype(jnp.bfloat16).reshape(
        clip_count, slab_len, 3, head_count, head_size
    )
    rates = jax.nn.sigmoid(
        jnp.dot(token_rows, rate_weight, preferred_element_type=jnp.float32) + rate_bias
    ) / (MB * (head_size + inner_width))
    rates = rates.reshape(clip_count, slab_len, head_count)
    gain_all = out_gain.reshape(head_count, head_size)
    length = lax.axis_size("seq")
    position = lax.axis_index("seq")
    turns = clip_count + length - 1
    received_start = (
        jnp.zeros((2, head_count, head_size, inner_width), jnp.bfloat16),
        jnp.zeros((head_count, inner_width), jnp.bfloat16),
        jnp.zeros((head_count, head_size), jnp.bfloat16),
    )
    outputs_start = jnp.zeros((clip_count, slab_len, head_count * head_size), jnp.bfloat16)
    own_state = (init_weights, init_bias_hidden, init_bias_out)

    def one_turn(turn_index, carry):
        received, outputs = carry
        unit_index = turn_index - position
        active = (unit_index >= 0) & (unit_index < clip_count)
        clip_index = jnp.clip(unit_index, 0, clip_count - 1)
        start_state = jax.tree.map(
            lambda member, other: jnp.where(position == 0, member, other.astype(jnp.float32)),
            own_state,
            received,
        )

        def run_unit(operands):
            entry_state, current = operands
            clip_block = lax.dynamic_index_in_dim(projected, clip_index, 0, keepdims=False)
            rate_block = lax.dynamic_index_in_dim(rates, clip_index, 0, keepdims=False)
            final_state, result = run_slab(entry_state, clip_block, rate_block, gain_all)
            current = lax.dynamic_update_slice(
                current, result[None], (clip_index, jnp.int32(0), jnp.int32(0))
            )
            return (jax.tree.map(lambda member: member.astype(jnp.bfloat16), final_state), current)

        def pass_through(operands):
            entry_state, current = operands
            return (jax.tree.map(lambda member: member.astype(jnp.bfloat16), entry_state), current)

        sent, outputs = lax.cond(active, run_unit, pass_through, (start_state, outputs))
        received = jax.tree.map(
            lambda part, own: part.astype(own.dtype), shifted(shortened(sent), "seq", 1), sent
        )
        return (received, outputs)

    unused, outputs = lax.fori_loop(0, turns, one_turn, (received_start, outputs_start))
    return outputs


def solution(mesh):
    return jax.shard_map(
        on_device,
        mesh=mesh,
        in_specs=(P("dp", "seq", None), P("dp", None), P(), P(), P(), P(), P(), P()),
        out_specs=P("dp", "seq", None),
        check_vma=False,
    )
```

profile of v0, /device:TPU:30, one launch (start us, length us, event | category | flops | bytes accessed | tf_op | source)
XLA Modules:
  0.0 1591.7 jit_solution(12472045964157043991)
XLA Ops:
  9.4 160.1 %all-gather.2.cloned.1.call-done = bf16[3072,4608]{1,0:T(8,128)(2,1)} async-done(((bf16[96,4608]{1,0:T(8,128)(2,1)}), bf16[3072,4608]{1,0:T(8,128)(2,1)}) %all-gather.2.cloned.1.call-update) | async-done | bytes 28311568 | tf_op jit(solution)/shard_map/all_gather | solution.py:107
  169.5 14.4 convolution_convert_fusion
  183.9 6.9 reshape.105
  190.9 6.4 copy.44
  199.6 1382.8 %while.36 = (s32[]{:T(128)}, bf16[2,24,64,256]{3,2,1,0:T(8,128)(2,1)}, bf16[24,256]{1,0:T(8,128)(2,1)S(1)}, bf16[24,64]{1,0:T(8,128)(2,1)S(1)}, bf16[2,128,1536]...) while((s32[]{:T(128)}, ...), condition=%wide.region_8.9_spmd, body=%wide.region_0.8_spmd.sunk | while | flops 2897933824 | bytes 141774256 | solution.py:159
  207.1 36.6 %collective-permute-done.2 = bf16[24,64]{1,0:T(8,128)(2,1)S(1)} collective-permute-done((bf16[24,64]{1,0:T(8,128)(2,1)S(1)}, bf16[24,64]{1,0:T(8,128)(2,1)S(1)}, u32[]{:S(2)}, u32[]{:S(2)}) %collective-permute-start.2) | collective-permute-done | bytes 3104 | tf_op jit(solution)/shard_map/while/body/eval_jaxpr/ppermute | solution.py:20
  252.2 35.8 %collective-permute-done.2 = bf16[24,64]{1,0:T(8,128)(2,1)S(1)} collective-permute-done((bf16[24,64]{1,0:T(8,128)(2,1)S(1)}, bf16[24,64]{1,0:T(8,128)(2,1)S(1)}, u32[]{:S(2)}, u32[]{:S(2)}) %collective-permute-start.2) | collective-permute-done | bytes 3104 | tf_op jit(solution)/shard_map/while/body/eval_jaxpr/ppermute | solution.py:20
  296.4 34.9 %collective-permute-done.2 = bf16[24,64]{1,0:T(8,128)(2,1)S(1)} collective-permute-done((bf16[24,64]{1,0:T(8,128)(2,1)S(1)}, bf16[24,64]{1,0:T(8,128)(2,1)S(1)}, u32[]{:S(2)}, u32[]{:S(2)}) %collective-permute-start.2) | collective-permute-done | bytes 3104 | tf_op jit(solution)/shard_map/while/body/eval_jaxpr/ppermute | solution.py:20
  339.7 34.8 %collective-permute-done.2 = bf16[24,64]{1,0:T(8,128)(2,1)S(1)} collective-permute-done((bf16[24,64]{1,0:T(8,128)(2,1)S(1)}, bf16[24,64]{1,0:T(8,128)(2,1)S(1)}, u32[]{:S(2)}, u32[]{:S(2)}) %collective-permute-start.2) | collective-permute-done | bytes 3104 | tf_op jit(solution)/shard_map/while/body/eval_jaxpr/ppermute | solution.py:20
  382.9 33.9 %collective-permute-done.2 = bf16[24,64]{1,0:T(8,128)(2,1)S(1)} collective-permute-done((bf16[24,64]{1,0:T(8,128)(2,1)S(1)}, bf16[24,64]{1,0:T(8,128)(2,1)S(1)}, u32[]{:S(2)}, u32[]{:S(2)}) %collective-permute-start.2) | collective-permute-done | bytes 3104 | tf_op jit(solution)/shard_map/while/body/eval_jaxpr/ppermute | solution.py:20
  425.3 33.0 %collective-permute-done.2 = bf16[24,64]{1,0:T(8,128)(2,1)S(1)} collective-permute-done((bf16[24,64]{1,0:T(8,128)(2,1)S(1)}, bf16[24,64]{1,0:T(8,128)(2,1)S(1)}, u32[]{:S(2)}, u32[]{:S(2)}) %collective-permute-start.2) | collective-permute-done | bytes 3104 | tf_op jit(solution)/shard_map/while/body/eval_jaxpr/ppermute | solution.py:20
  466.7 809.2 %collective-permute-done.2 = bf16[24,64]{1,0:T(8,128)(2,1)S(1)} collective-permute-done((bf16[24,64]{1,0:T(8,128)(2,1)S(1)}, bf16[24,64]{1,0:T(8,128)(2,1)S(1)}, u32[]{:S(2)}, u32[]{:S(2)}) %collective-permute-start.2) | collective-permute-done | bytes 3104 | tf_op jit(solution)/shard_map/while/body/eval_jaxpr/ppermute | solution.py:20
  1279.0 112.1 %conditional.2 = ((bf16[2,128,1536]{1,2,0:T(8,128)(2,1)}, f32[2,24,64,256]{3,2,1,0:T(8,128)S(1)}, f32[24,256]{1,0:T(8,128)S(1)}, f32[24,64]{1,0:T(8,128)S(1)})) conditional(s32[]{:T(128)} %convert_element_type.81, (bf16[2,128,1536]{1,2,0:T(8,128)(2,1)}, f32[2,24,64,256]{3,2,1,0:T(8,128)S(1)}, f32[24,256]{1,0:T(8,128)S(1)}, ...), branch_computations={%region_1.1_spmd, %region_2.7_spmd} | conditional | flops 2895551488 | bytes 116423672 | solution.py:153
  1282.1 5.8 reshape.104
  1291.8 88.4 %while.35 = (s32[]{:T(128)}, f32[2,24,64,256]{3,2,1,0:T(8,128)S(1)}, f32[24,256]{1,0:T(8,128)S(1)}, f32[24,64]{1,0:T(8,128)S(1)}, f32[2,24,64,64]{3,2,1,0:T(8,12...) while((s32[]{:T(128)}, ...), condition=%wide.region_6.5_spmd, body=%wide.region_3.4_spmd.sunk | while | flops 2893975552 | bytes 98181968 | solution.py:82
  1331.1 4.5 fusion.140
  1375.3 4.5 fusion.140
  1396.4 33.0 %collective-permute-done.2 = bf16[24,64]{1,0:T(8,128)(2,1)S(1)} collective-permute-done((bf16[24,64]{1,0:T(8,128)(2,1)S(1)}, bf16[24,64]{1,0:T(8,128)(2,1)S(1)}, u32[]{:S(2)}, u32[]{:S(2)}) %collective-permute-start.2) | collective-permute-done | bytes 3104 | tf_op jit(solution)/shard_map/while/body/eval_jaxpr/ppermute | solution.py:20
  1432.5 112.1 %conditional.2 = ((bf16[2,128,1536]{1,2,0:T(8,128)(2,1)}, f32[2,24,64,256]{3,2,1,0:T(8,128)S(1)}, f32[24,256]{1,0:T(8,128)S(1)}, f32[24,64]{1,0:T(8,128)S(1)})) conditional(s32[]{:T(128)} %convert_element_type.81, (bf16[2,128,1536]{1,2,0:T(8,128)(2,1)}, f32[2,24,64,256]{3,2,1,0:T(8,128)S(1)}, f32[24,256]{1,0:T(8,128)S(1)}, ...), branch_computations={%region_1.1_spmd, %region_2.7_spmd} | conditional | flops 2895551488 | bytes 116423672 | solution.py:153
  1435.6 5.8 reshape.104
  1445.3 88.4 %while.35 = (s32[]{:T(128)}, f32[2,24,64,256]{3,2,1,0:T(8,128)S(1)}, f32[24,256]{1,0:T(8,128)S(1)}, f32[24,64]{1,0:T(8,128)S(1)}, f32[2,24,64,64]{3,2,1,0:T(8,12...) while((s32[]{:T(128)}, ...), condition=%wide.region_6.5_spmd, body=%wide.region_3.4_spmd.sunk | while | flops 2893975552 | bytes 98181968 | solution.py:82
  1484.6 4.5 fusion.140
  1528.8 4.5 fusion.140
  1549.9 31.4 %collective-permute-done.2 = bf16[24,64]{1,0:T(8,128)(2,1)S(1)} collective-permute-done((bf16[24,64]{1,0:T(8,128)(2,1)S(1)}, bf16[24,64]{1,0:T(8,128)(2,1)S(1)}, u32[]{:S(2)}, u32[]{:S(2)}) %collective-permute-start.2) | collective-permute-done | bytes 3104 | tf_op jit(solution)/shard_map/while/body/eval_jaxpr/ppermute | solution.py:20
  (315 shorter events, 276.4 us)
Async XLA Ops:
  6.5 163.0 %all-gather.2.cloned.1.call-start = ((), (), s32[]{:S(2)}) async-start(), calls=%async_computation | async-start | bytes 29196288 | tf_op jit(solution)/shard_map/all_gather | solution.py:107
  203.2 40.5 %collective-permute-start = (bf16[2,24,64,256]{3,2,1,0:T(8,128)(2,1)}, bf16[2,24,64,256]{3,2,1,0:T(8,128)(2,1)S(1)}, u32[]{:S(2)}, u32[]{:S(2)}) collective-permute-start(bf16[2,24,64,256]{3,2,1,0:T(8,128)(2,1)} %convert_element_type.82), channel_id=1, source_target_pairs={{0,32},{32,64},{64,96},{96,128},{128,160},{160,192},{192,224},{1,3... | collective-permute-start | bytes 4718600 | tf_op jit(solution)/shard_map/while/body/eval_jaxpr/ppermute | solution.py:20
  204.5 39.2 %collective-permute-start.1 = (bf16[24,256]{1,0:T(8,128)(2,1)S(1)}, bf16[24,256]{1,0:T(8,128)(2,1)S(1)}, u32[]{:S(2)}, u32[]{:S(2)}) collective-permute-start(bf16[24,256]{1,0:T(8,128)(2,1)S(1)} %convert_element_type.83), channel_id=1, source_target_pairs={{0,32},{32,64},{64,96},{96,128},{128,160},{160,192},{192,224},{1,3... | collective-permute-start | bytes 36872 | tf_op jit(solution)/shard_map/while/body/eval_jaxpr/ppermute | solution.py:20
  205.8 37.9 %collective-permute-start.2 = (bf16[24,64]{1,0:T(8,128)(2,1)S(1)}, bf16[24,64]{1,0:T(8,128)(2,1)S(1)}, u32[]{:S(2)}, u32[]{:S(2)}) collective-permute-start(bf16[24,64]{1,0:T(8,128)(2,1)S(1)} %convert_element_type.84), channel_id=1, source_target_pairs={{0,32},{32,64},{64,96},{96,128},{128,160},{160,192},{192,224},{1,3... | collective-permute-start | bytes 9224 | tf_op jit(solution)/shard_map/while/body/eval_jaxpr/ppermute | solution.py:20
  248.2 39.7 %collective-permute-start = (bf16[2,24,64,256]{3,2,1,0:T(8,128)(2,1)}, bf16[2,24,64,256]{3,2,1,0:T(8,128)(2,1)S(1)}, u32[]{:S(2)}, u32[]{:S(2)}) collective-permute-start(bf16[2,24,64,256]{3,2,1,0:T(8,128)(2,1)} %convert_element_type.82), channel_id=1, source_target_pairs={{0,32},{32,64},{64,96},{96,128},{128,160},{160,192},{192,224},{1,3... | collective-permute-start | bytes 4718600 | tf_op jit(solution)/shard_map/while/body/eval_jaxpr/ppermute | solution.py:20
  249.5 38.4 %collective-permute-start.1 = (bf16[24,256]{1,0:T(8,128)(2,1)S(1)}, bf16[24,256]{1,0:T(8,128)(2,1)S(1)}, u32[]{:S(2)}, u32[]{:S(2)}) collective-permute-start(bf16[24,256]{1,0:T(8,128)(2,1)S(1)} %convert_element_type.83), channel_id=1, source_target_pairs={{0,32},{32,64},{64,96},{96,128},{128,160},{160,192},{192,224},{1,3... | collective-permute-start | bytes 36872 | tf_op jit(solution)/shard_map/while/body/eval_jaxpr/ppermute | solution.py:20
  250.8 37.1 %collective-permute-start.2 = (bf16[24,64]{1,0:T(8,128)(2,1)S(1)}, bf16[24,64]{1,0:T(8,128)(2,1)S(1)}, u32[]{:S(2)}, u32[]{:S(2)}) collective-permute-start(bf16[24,64]{1,0:T(8,128)(2,1)S(1)} %convert_element_type.84), channel_id=1, source_target_pairs={{0,32},{32,64},{64,96},{96,128},{128,160},{160,192},{192,224},{1,3... | collective-permute-start | bytes 9224 | tf_op jit(solution)/shard_map/while/body/eval_jaxpr/ppermute | solution.py:20
  292.5 38.8 %collective-permute-start = (bf16[2,24,64,256]{3,2,1,0:T(8,128)(2,1)}, bf16[2,24,64,256]{3,2,1,0:T(8,128)(2,1)S(1)}, u32[]{:S(2)}, u32[]{:S(2)}) collective-permute-start(bf16[2,24,64,256]{3,2,1,0:T(8,128)(2,1)} %convert_element_type.82), channel_id=1, source_target_pairs={{0,32},{32,64},{64,96},{96,128},{128,160},{160,192},{192,224},{1,3... | collective-permute-start | bytes 4718600 | tf_op jit(solution)/shard_map/while/body/eval_jaxpr/ppermute | solution.py:20
  293.8 37.5 %collective-permute-start.1 = (bf16[24,256]{1,0:T(8,128)(2,1)S(1)}, bf16[24,256]{1,0:T(8,128)(2,1)S(1)}, u32[]{:S(2)}, u32[]{:S(2)}) collective-permute-start(bf16[24,256]{1,0:T(8,128)(2,1)S(1)} %convert_element_type.83), channel_id=1, source_target_pairs={{0,32},{32,64},{64,96},{96,128},{128,160},{160,192},{192,224},{1,3... | collective-permute-start | bytes 36872 | tf_op jit(solution)/shard_map/while/body/eval_jaxpr/ppermute | solution.py:20
  295.1 36.2 %collective-permute-start.2 = (bf16[24,64]{1,0:T(8,128)(2,1)S(1)}, bf16[24,64]{1,0:T(8,128)(2,1)S(1)}, u32[]{:S(2)}, u32[]{:S(2)}) collective-permute-start(bf16[24,64]{1,0:T(8,128)(2,1)S(1)} %convert_element_type.84), channel_id=1, source_target_pairs={{0,32},{32,64},{64,96},{96,128},{128,160},{160,192},{192,224},{1,3... | collective-permute-start | bytes 9224 | tf_op jit(solution)/shard_map/while/body/eval_jaxpr/ppermute | solution.py:20
  335.8 38.8 %collective-permute-start = (bf16[2,24,64,256]{3,2,1,0:T(8,128)(2,1)}, bf16[2,24,64,256]{3,2,1,0:T(8,128)(2,1)S(1)}, u32[]{:S(2)}, u32[]{:S(2)}) collective-permute-start(bf16[2,24,64,256]{3,2,1,0:T(8,128)(2,1)} %convert_element_type.82), channel_id=1, source_target_pairs={{0,32},{32,64},{64,96},{96,128},{128,160},{160,192},{192,224},{1,3... | collective-permute-start | bytes 4718600 | tf_op jit(solution)/shard_map/while/body/eval_jaxpr/ppermute | solution.py:20
  337.1 37.4 %collective-permute-start.1 = (bf16[24,256]{1,0:T(8,128)(2,1)S(1)}, bf16[24,256]{1,0:T(8,128)(2,1)S(1)}, u32[]{:S(2)}, u32[]{:S(2)}) collective-permute-start(bf16[24,256]{1,0:T(8,128)(2,1)S(1)} %convert_element_type.83), channel_id=1, source_target_pairs={{0,32},{32,64},{64,96},{96,128},{128,160},{160,192},{192,224},{1,3... | collective-permute-start | bytes 36872 | tf_op jit(solution)/shard_map/while/body/eval_jaxpr/ppermute | solution.py:20
  338.4 36.1 %collective-permute-start.2 = (bf16[24,64]{1,0:T(8,128)(2,1)S(1)}, bf16[24,64]{1,0:T(8,128)(2,1)S(1)}, u32[]{:S(2)}, u32[]{:S(2)}) collective-permute-start(bf16[24,64]{1,0:T(8,128)(2,1)S(1)} %convert_element_type.84), channel_id=1, source_target_pairs={{0,32},{32,64},{64,96},{96,128},{128,160},{160,192},{192,224},{1,3... | collective-permute-start | bytes 9224 | tf_op jit(solution)/shard_map/while/body/eval_jaxpr/ppermute | solution.py:20
  379.0 37.9 %collective-permute-start = (bf16[2,24,64,256]{3,2,1,0:T(8,128)(2,1)}, bf16[2,24,64,256]{3,2,1,0:T(8,128)(2,1)S(1)}, u32[]{:S(2)}, u32[]{:S(2)}) collective-permute-start(bf16[2,24,64,256]{3,2,1,0:T(8,128)(2,1)} %convert_element_type.82), channel_id=1, source_target_pairs={{0,32},{32,64},{64,96},{96,128},{128,160},{160,192},{192,224},{1,3... | collective-permute-start | bytes 4718600 | tf_op jit(solution)/shard_map/while/body/eval_jaxpr/ppermute | solution.py:20
  380.3 36.6 %collective-permute-start.1 = (bf16[24,256]{1,0:T(8,128)(2,1)S(1)}, bf16[24,256]{1,0:T(8,128)(2,1)S(1)}, u32[]{:S(2)}, u32[]{:S(2)}) collective-permute-start(bf16[24,256]{1,0:T(8,128)(2,1)S(1)} %convert_element_type.83), channel_id=1, source_target_pairs={{0,32},{32,64},{64,96},{96,128},{128,160},{160,192},{192,224},{1,3... | collective-permute-start | bytes 36872 | tf_op jit(solution)/shard_map/while/body/eval_jaxpr/ppermute | solution.py:20
  381.6 35.2 %collective-permute-start.2 = (bf16[24,64]{1,0:T(8,128)(2,1)S(1)}, bf16[24,64]{1,0:T(8,128)(2,1)S(1)}, u32[]{:S(2)}, u32[]{:S(2)}) collective-permute-start(bf16[24,64]{1,0:T(8,128)(2,1)S(1)} %convert_element_type.84), channel_id=1, source_target_pairs={{0,32},{32,64},{64,96},{96,128},{128,160},{160,192},{192,224},{1,3... | collective-permute-start | bytes 9224 | tf_op jit(solution)/shard_map/while/body/eval_jaxpr/ppermute | solution.py:20
  421.4 36.9 %collective-permute-start = (bf16[2,24,64,256]{3,2,1,0:T(8,128)(2,1)}, bf16[2,24,64,256]{3,2,1,0:T(8,128)(2,1)S(1)}, u32[]{:S(2)}, u32[]{:S(2)}) collective-permute-start(bf16[2,24,64,256]{3,2,1,0:T(8,128)(2,1)} %convert_element_type.82), channel_id=1, source_target_pairs={{0,32},{32,64},{64,96},{96,128},{128,160},{160,192},{192,224},{1,3... | collective-permute-start | bytes 4718600 | tf_op jit(solution)/shard_map/while/body/eval_jaxpr/ppermute | solution.py:20
  422.7 35.6 %collective-permute-start.1 = (bf16[24,256]{1,0:T(8,128)(2,1)S(1)}, bf16[24,256]{1,0:T(8,128)(2,1)S(1)}, u32[]{:S(2)}, u32[]{:S(2)}) collective-permute-start(bf16[24,256]{1,0:T(8,128)(2,1)S(1)} %convert_element_type.83), channel_id=1, source_target_pairs={{0,32},{32,64},{64,96},{96,128},{128,160},{160,192},{192,224},{1,3... | collective-permute-start | bytes 36872 | tf_op jit(solution)/shard_map/while/body/eval_jaxpr/ppermute | solution.py:20
  462.8 813.1 %collective-permute-start = (bf16[2,24,64,256]{3,2,1,0:T(8,128)(2,1)}, bf16[2,24,64,256]{3,2,1,0:T(8,128)(2,1)S(1)}, u32[]{:S(2)}, u32[]{:S(2)}) collective-permute-start(bf16[2,24,64,256]{3,2,1,0:T(8,128)(2,1)} %convert_element_type.82), channel_id=1, source_target_pairs={{0,32},{32,64},{64,96},{96,128},{128,160},{160,192},{192,224},{1,3... | collective-permute-start | bytes 4718600 | tf_op jit(solution)/shard_map/while/body/eval_jaxpr/ppermute | solution.py:20
  464.1 811.8 %collective-permute-start.1 = (bf16[24,256]{1,0:T(8,128)(2,1)S(1)}, bf16[24,256]{1,0:T(8,128)(2,1)S(1)}, u32[]{:S(2)}, u32[]{:S(2)}) collective-permute-start(bf16[24,256]{1,0:T(8,128)(2,1)S(1)} %convert_element_type.83), channel_id=1, source_target_pairs={{0,32},{32,64},{64,96},{96,128},{128,160},{160,192},{192,224},{1,3... | collective-permute-start | bytes 36872 | tf_op jit(solution)/shard_map/while/body/eval_jaxpr/ppermute | solution.py:20
  465.4 810.5 %collective-permute-start.2 = (bf16[24,64]{1,0:T(8,128)(2,1)S(1)}, bf16[24,64]{1,0:T(8,128)(2,1)S(1)}, u32[]{:S(2)}, u32[]{:S(2)}) collective-permute-start(bf16[24,64]{1,0:T(8,128)(2,1)S(1)} %convert_element_type.84), channel_id=1, source_target_pairs={{0,32},{32,64},{64,96},{96,128},{128,160},{160,192},{192,224},{1,3... | collective-permute-start | bytes 9224 | tf_op jit(solution)/shard_map/while/body/eval_jaxpr/ppermute | solution.py:20
  1392.5 36.9 %collective-permute-start = (bf16[2,24,64,256]{3,2,1,0:T(8,128)(2,1)}, bf16[2,24,64,256]{3,2,1,0:T(8,128)(2,1)S(1)}, u32[]{:S(2)}, u32[]{:S(2)}) collective-permute-start(bf16[2,24,64,256]{3,2,1,0:T(8,128)(2,1)} %convert_element_type.82), channel_id=1, source_target_pairs={{0,32},{32,64},{64,96},{96,128},{128,160},{160,192},{192,224},{1,3... | collective-permute-start | bytes 4718600 | tf_op jit(solution)/shard_map/while/body/eval_jaxpr/ppermute | solution.py:20
  1393.8 35.6 %collective-permute-start.1 = (bf16[24,256]{1,0:T(8,128)(2,1)S(1)}, bf16[24,256]{1,0:T(8,128)(2,1)S(1)}, u32[]{:S(2)}, u32[]{:S(2)}) collective-permute-start(bf16[24,256]{1,0:T(8,128)(2,1)S(1)} %convert_element_type.83), channel_id=1, source_target_pairs={{0,32},{32,64},{64,96},{96,128},{128,160},{160,192},{192,224},{1,3... | collective-permute-start | bytes 36872 | tf_op jit(solution)/shard_map/while/body/eval_jaxpr/ppermute | solution.py:20
  1546.0 35.3 %collective-permute-start = (bf16[2,24,64,256]{3,2,1,0:T(8,128)(2,1)}, bf16[2,24,64,256]{3,2,1,0:T(8,128)(2,1)S(1)}, u32[]{:S(2)}, u32[]{:S(2)}) collective-permute-start(bf16[2,24,64,256]{3,2,1,0:T(8,128)(2,1)} %convert_element_type.82), channel_id=1, source_target_pairs={{0,32},{32,64},{64,96},{96,128},{128,160},{160,192},{192,224},{1,3... | collective-permute-start | bytes 4718600 | tf_op jit(solution)/shard_map/while/body/eval_jaxpr/ppermute | solution.py:20
  (50 other events, 243.9 us)
Sparse Core Ops, SparseCore 0:
  9.2 160.2 all-gather.1
where the time goes:
time: 1590 us
  waiting for transfers between devices  1240 us (78%)
  local copies, waits for them, and re-layouts  124 us (8%)
  matrix products  122 us (8%)
  other arithmetic  52 us (3%)
  starting transfers between devices  34.8 us (2%)
    ppermute x27, waiting for transfers between devices, shifted(): return lax.ppermute(block, axis, route)  1080 us
    all_gather x1, waiting for transfers between devices, on_device(): full_weight = lax.all_gather(proj_weight, 'dp', axis=0, tiled=True)  160 us
    dynamic_slice x24, local copies, waits for them, and re-layouts, run_slab(): lax.scan(minibatch, start_state, (inputs[0], inputs[1], inputs[2], step_r...  56.4 us
    ppermute x27, starting transfers between devices, shifted(): return lax.ppermute(block, axis, route)  34.8 us
  transfers between devices with their start and end apart: 28, of which 10 were waited for; matrix products, arithmetic and copies ran while one was open for 0% of the time, Pallas kernels for 0%

commit v1 on v0

--- a/solution.py
+++ b/solution.py
@@ -1,3 +1,4 @@
+import functools
 import math
 import jax
 import jax.numpy as jnp
@@ -8,6 +9,15 @@
 precise = lax.Precision.HIGHEST
 coefficient = 0.044715
 root_scale = math.sqrt(2.0 / math.pi)
+
+
+def link_slabs_all(piece_in, net_axis):
+    return jnp.concatenate(
+        lax.all_to_all(jnp.stack([piece_in] * lax.axis_size(net_axis)), net_axis, 0, 0), axis=0
+    )
+
+
+show_masks_on = functools.partial(link_slabs_all, net_axis="dp")
 
 
 def shortened(x):
@@ -104,7 +114,7 @@
     head_size = init_weights.shape[2]
     inner_width = init_weights.shape[3]
     token_rows = frames.reshape(clip_count * slab_len, model_width)
-    full_weight = lax.all_gather(proj_weight, "dp", axis=0, tiled=True)
+    full_weight = show_masks_on(proj_weight)
     projected = jnp.dot(token_rows, full_weight, preferred_element_type=jnp.float32)
     projected = projected.astype(jnp.bfloat16).reshape(
         clip_count, slab_len, 3, head_count, head_size

time: 1590 us -> 2050 us (1.29)
  the two profiles are of different devices: /device:TPU:30 before, /device:TPU:126 now
where the time goes in v1:
time: 2050 us
  waiting for transfers between devices  1700 us (83%)
  local copies, waits for them, and re-layouts  130 us (6%)
  matrix products  121 us (6%)
  other arithmetic  53.9 us (3%)
  starting transfers between devices  43.7 us (2%)
    ppermute x27, waiting for transfers between devices, shifted(): return lax.ppermute(block, axis, route)  1060 us
    all_to_all x1, waiting for transfers between devices, link_slabs_all(): lax.all_to_all(jnp.stack([piece_in] * lax.axis_size(net_axis)), net_axis,...  634 us
    dynamic_slice x24, local copies, waits for them, and re-layouts, run_slab(): lax.scan(minibatch, start_state, (inputs[0], inputs[1], inputs[2], step_r...  56.4 us
  transfers between devices with their start and end apart: 28, of which 10 were waited for; matrix products, arithmetic and copies ran while one was open for 0% of the time, Pallas kernels for 0%

profile of v1, /device:TPU:126, one launch (start us, length us, event | category | flops | bytes accessed | tf_op | source)
XLA Modules:
  0.0 2048.9 jit_solution(13671718152490009081)
XLA Ops:
  0.0 10.5 stack.8
  10.5 8.9 all-to-all-start
  20.1 633.7 %all-to-all-done = bf16[32,96,4608]{2,1,0:T(8,128)(2,1)} async-done(((bf16[32,96,4608]{2,1,0:T(8,128)(2,1)}), bf16[32,96,4608]{2,1,0:T(8,128)(2,1)}, u32[]{:S(2)}, u32[]{:S(2)}) %all-to-all-start) | async-done | bytes 28311584 | tf_op jit(solution)/shard_map/all_to_all | solution.py:16
  653.8 14.4 convolution_convert_fusion
  668.1 6.9 reshape.111
  675.1 6.4 copy.44
  683.8 1362.6 %while.36 = (s32[]{:T(128)}, bf16[2,24,64,256]{3,2,1,0:T(8,128)(2,1)}, bf16[24,256]{1,0:T(8,128)(2,1)S(1)}, bf16[24,64]{1,0:T(8,128)(2,1)S(1)}, bf16[2,128,1536]...) while((s32[]{:T(128)}, ...), condition=%wide.region_8.9_spmd, body=%wide.region_0.8_spmd.sunk | while | flops 2897933824 | bytes 141774256 | solution.py:169
  691.5 36.0 %collective-permute-done.2 = bf16[24,64]{1,0:T(8,128)(2,1)S(1)} collective-permute-done((bf16[24,64]{1,0:T(8,128)(2,1)S(1)}, bf16[24,64]{1,0:T(8,128)(2,1)S(1)}, u32[]{:S(2)}, u32[]{:S(2)}) %collective-permute-start.2) | collective-permute-done | bytes 3104 | tf_op jit(solution)/shard_map/while/body/eval_jaxpr/ppermute | solution.py:30
  736.2 35.1 %collective-permute-done.2 = bf16[24,64]{1,0:T(8,128)(2,1)S(1)} collective-permute-done((bf16[24,64]{1,0:T(8,128)(2,1)S(1)}, bf16[24,64]{1,0:T(8,128)(2,1)S(1)}, u32[]{:S(2)}, u32[]{:S(2)}) %collective-permute-start.2) | collective-permute-done | bytes 3104 | tf_op jit(solution)/shard_map/while/body/eval_jaxpr/ppermute | solution.py:30
  779.9 34.2 %collective-permute-done.2 = bf16[24,64]{1,0:T(8,128)(2,1)S(1)} collective-permute-done((bf16[24,64]{1,0:T(8,128)(2,1)S(1)}, bf16[24,64]{1,0:T(8,128)(2,1)S(1)}, u32[]{:S(2)}, u32[]{:S(2)}) %collective-permute-start.2) | collective-permute-done | bytes 3104 | tf_op jit(solution)/shard_map/while/body/eval_jaxpr/ppermute | solution.py:30
  822.8 34.0 %collective-permute-done.2 = bf16[24,64]{1,0:T(8,128)(2,1)S(1)} collective-permute-done((bf16[24,64]{1,0:T(8,128)(2,1)S(1)}, bf16[24,64]{1,0:T(8,128)(2,1)S(1)}, u32[]{:S(2)}, u32[]{:S(2)}) %collective-permute-start.2) | collective-permute-done | bytes 3104 | tf_op jit(solution)/shard_map/while/body/eval_jaxpr/ppermute | solution.py:30
  865.4 33.2 %collective-permute-done.2 = bf16[24,64]{1,0:T(8,128)(2,1)S(1)} collective-permute-done((bf16[24,64]{1,0:T(8,128)(2,1)S(1)}, bf16[24,64]{1,0:T(8,128)(2,1)S(1)}, u32[]{:S(2)}, u32[]{:S(2)}) %collective-permute-start.2) | collective-permute-done | bytes 3104 | tf_op jit(solution)/shard_map/while/body/eval_jaxpr/ppermute | solution.py:30
  907.3 32.3 %collective-permute-done.2 = bf16[24,64]{1,0:T(8,128)(2,1)S(1)} collective-permute-done((bf16[24,64]{1,0:T(8,128)(2,1)S(1)}, bf16[24,64]{1,0:T(8,128)(2,1)S(1)}, u32[]{:S(2)}, u32[]{:S(2)}) %collective-permute-start.2) | collective-permute-done | bytes 3104 | tf_op jit(solution)/shard_map/while/body/eval_jaxpr/ppermute | solution.py:30
  948.2 796.2 %collective-permute-done.2 = bf16[24,64]{1,0:T(8,128)(2,1)S(1)} collective-permute-done((bf16[24,64]{1,0:T(8,128)(2,1)S(1)}, bf16[24,64]{1,0:T(8,128)(2,1)S(1)}, u32[]{:S(2)}, u32[]{:S(2)}) %collective-permute-start.2) | collective-permute-done | bytes 3104 | tf_op jit(solution)/shard_map/while/body/eval_jaxpr/ppermute | solution.py:30
  1747.7 110.4 %conditional.2 = ((bf16[2,128,1536]{1,2,0:T(8,128)(2,1)}, f32[2,24,64,256]{3,2,1,0:T(8,128)S(1)}, f32[24,256]{1,0:T(8,128)S(1)}, f32[24,64]{1,0:T(8,128)S(1)})) conditional(s32[]{:T(128)} %convert_element_type.81, (bf16[2,128,1536]{1,2,0:T(8,128)(2,1)}, f32[2,24,64,256]{3,2,1,0:T(8,128)S(1)}, f32[24,256]{1,0:T(8,128)S(1)}, ...), branch_computations={%region_1.1_spmd, %region_2.7_spmd} | conditional | flops 2895551488 | bytes 116423672 | solution.py:163
  1750.8 5.8 reshape.110
  1760.5 86.7 %while.35 = (s32[]{:T(128)}, f32[2,24,64,256]{3,2,1,0:T(8,128)S(1)}, f32[24,256]{1,0:T(8,128)S(1)}, f32[24,64]{1,0:T(8,128)S(1)}, f32[2,24,64,64]{3,2,1,0:T(8,12...) while((s32[]{:T(128)}, ...), condition=%wide.region_6.5_spmd, body=%wide.region_3.4_spmd.sunk | while | flops 2893975552 | bytes 98181968 | solution.py:92
  1842.3 4.5 fusion.140
  1863.4 32.2 %collective-permute-done.2 = bf16[24,64]{1,0:T(8,128)(2,1)S(1)} collective-permute-done((bf16[24,64]{1,0:T(8,128)(2,1)S(1)}, bf16[24,64]{1,0:T(8,128)(2,1)S(1)}, u32[]{:S(2)}, u32[]{:S(2)}) %collective-permute-start.2) | collective-permute-done | bytes 3104 | tf_op jit(solution)/shard_map/while/body/eval_jaxpr/ppermute | solution.py:30
  1898.9 110.4 %conditional.2 = ((bf16[2,128,1536]{1,2,0:T(8,128)(2,1)}, f32[2,24,64,256]{3,2,1,0:T(8,128)S(1)}, f32[24,256]{1,0:T(8,128)S(1)}, f32[24,64]{1,0:T(8,128)S(1)})) conditional(s32[]{:T(128)} %convert_element_type.81, (bf16[2,128,1536]{1,2,0:T(8,128)(2,1)}, f32[2,24,64,256]{3,2,1,0:T(8,128)S(1)}, f32[24,256]{1,0:T(8,128)S(1)}, ...), branch_computations={%region_1.1_spmd, %region_2.7_spmd} | conditional | flops 2895551488 | bytes 116423672 | solution.py:163
  1902.0 5.8 reshape.110
  1911.7 86.7 %while.35 = (s32[]{:T(128)}, f32[2,24,64,256]{3,2,1,0:T(8,128)S(1)}, f32[24,256]{1,0:T(8,128)S(1)}, f32[24,64]{1,0:T(8,128)S(1)}, f32[2,24,64,64]{3,2,1,0:T(8,12...) while((s32[]{:T(128)}, ...), condition=%wide.region_6.5_spmd, body=%wide.region_3.4_spmd.sunk | while | flops 2893975552 | bytes 98181968 | solution.py:92
  1993.5 4.5 fusion.140
  2014.6 30.7 %collective-permute-done.2 = bf16[24,64]{1,0:T(8,128)(2,1)S(1)} collective-permute-done((bf16[24,64]{1,0:T(8,128)(2,1)S(1)}, bf16[24,64]{1,0:T(8,128)(2,1)S(1)}, u32[]{:S(2)}, u32[]{:S(2)}) %collective-permute-start.2) | collective-permute-done | bytes 3104 | tf_op jit(solution)/shard_map/while/body/eval_jaxpr/ppermute | solution.py:30
  (319 shorter events, 281.5 us)
Async XLA Ops:
  10.5 643.2 %all-to-all-start = ((bf16[32,96,4608]{2,1,0:T(8,128)(2,1)}), bf16[32,96,4608]{2,1,0:T(8,128)(2,1)}, u32[]{:S(2)}, u32[]{:S(2)}) async-start(bf16[32,96,4608]{2,1,0:T(8,128)(2,1)} %stack.8), calls=%async_computation | async-start | bytes 56623104 | tf_op jit(solution)/shard_map/all_to_all | solution.py:16
  687.6 39.9 %collective-permute-start = (bf16[2,24,64,256]{3,2,1,0:T(8,128)(2,1)}, bf16[2,24,64,256]{3,2,1,0:T(8,128)(2,1)S(1)}, u32[]{:S(2)}, u32[]{:S(2)}) collective-permute-start(bf16[2,24,64,256]{3,2,1,0:T(8,128)(2,1)} %convert_element_type.82), channel_id=1, source_target_pairs={{0,32},{32,64},{64,96},{96,128},{128,160},{160,192},{192,224},{1,3... | collective-permute-start | bytes 4718600 | tf_op jit(solution)/shard_map/while/body/eval_jaxpr/ppermute | solution.py:30
  688.9 38.6 %collective-permute-start.1 = (bf16[24,256]{1,0:T(8,128)(2,1)S(1)}, bf16[24,256]{1,0:T(8,128)(2,1)S(1)}, u32[]{:S(2)}, u32[]{:S(2)}) collective-permute-start(bf16[24,256]{1,0:T(8,128)(2,1)S(1)} %convert_element_type.83), channel_id=1, source_target_pairs={{0,32},{32,64},{64,96},{96,128},{128,160},{160,192},{192,224},{1,3... | collective-permute-start | bytes 36872 | tf_op jit(solution)/shard_map/while/body/eval_jaxpr/ppermute | solution.py:30
  690.2 37.3 %collective-permute-start.2 = (bf16[24,64]{1,0:T(8,128)(2,1)S(1)}, bf16[24,64]{1,0:T(8,128)(2,1)S(1)}, u32[]{:S(2)}, u32[]{:S(2)}) collective-permute-start(bf16[24,64]{1,0:T(8,128)(2,1)S(1)} %convert_element_type.84), channel_id=1, source_target_pairs={{0,32},{32,64},{64,96},{96,128},{128,160},{160,192},{192,224},{1,3... | collective-permute-start | bytes 9224 | tf_op jit(solution)/shard_map/while/body/eval_jaxpr/ppermute | solution.py:30
  732.3 39.0 %collective-permute-start = (bf16[2,24,64,256]{3,2,1,0:T(8,128)(2,1)}, bf16[2,24,64,256]{3,2,1,0:T(8,128)(2,1)S(1)}, u32[]{:S(2)}, u32[]{:S(2)}) collective-permute-start(bf16[2,24,64,256]{3,2,1,0:T(8,128)(2,1)} %convert_element_type.82), channel_id=1, source_target_pairs={{0,32},{32,64},{64,96},{96,128},{128,160},{160,192},{192,224},{1,3... | collective-permute-start | bytes 4718600 | tf_op jit(solution)/shard_map/while/body/eval_jaxpr/ppermute | solution.py:30
  733.6 37.7 %collective-permute-start.1 = (bf16[24,256]{1,0:T(8,128)(2,1)S(1)}, bf16[24,256]{1,0:T(8,128)(2,1)S(1)}, u32[]{:S(2)}, u32[]{:S(2)}) collective-permute-start(bf16[24,256]{1,0:T(8,128)(2,1)S(1)} %convert_element_type.83), channel_id=1, source_target_pairs={{0,32},{32,64},{64,96},{96,128},{128,160},{160,192},{192,224},{1,3... | collective-permute-start | bytes 36872 | tf_op jit(solution)/shard_map/while/body/eval_jaxpr/ppermute | solution.py:30
  734.9 36.4 %collective-permute-start.2 = (bf16[24,64]{1,0:T(8,128)(2,1)S(1)}, bf16[24,64]{1,0:T(8,128)(2,1)S(1)}, u32[]{:S(2)}, u32[]{:S(2)}) collective-permute-start(bf16[24,64]{1,0:T(8,128)(2,1)S(1)} %convert_element_type.84), channel_id=1, source_target_pairs={{0,32},{32,64},{64,96},{96,128},{128,160},{160,192},{192,224},{1,3... | collective-permute-start | bytes 9224 | tf_op jit(solution)/shard_map/while/body/eval_jaxpr/ppermute | solution.py:30
  776.0 38.1 %collective-permute-start = (bf16[2,24,64,256]{3,2,1,0:T(8,128)(2,1)}, bf16[2,24,64,256]{3,2,1,0:T(8,128)(2,1)S(1)}, u32[]{:S(2)}, u32[]{:S(2)}) collective-permute-start(bf16[2,24,64,256]{3,2,1,0:T(8,128)(2,1)} %convert_element_type.82), channel_id=1, source_target_pairs={{0,32},{32,64},{64,96},{96,128},{128,160},{160,192},{192,224},{1,3... | collective-permute-start | bytes 4718600 | tf_op jit(solution)/shard_map/while/body/eval_jaxpr/ppermute | solution.py:30
  777.3 36.8 %collective-permute-start.1 = (bf16[24,256]{1,0:T(8,128)(2,1)S(1)}, bf16[24,256]{1,0:T(8,128)(2,1)S(1)}, u32[]{:S(2)}, u32[]{:S(2)}) collective-permute-start(bf16[24,256]{1,0:T(8,128)(2,1)S(1)} %convert_element_type.83), channel_id=1, source_target_pairs={{0,32},{32,64},{64,96},{96,128},{128,160},{160,192},{192,224},{1,3... | collective-permute-start | bytes 36872 | tf_op jit(solution)/shard_map/while/body/eval_jaxpr/ppermute | solution.py:30
  778.6 35.5 %collective-permute-start.2 = (bf16[24,64]{1,0:T(8,128)(2,1)S(1)}, bf16[24,64]{1,0:T(8,128)(2,1)S(1)}, u32[]{:S(2)}, u32[]{:S(2)}) collective-permute-start(bf16[24,64]{1,0:T(8,128)(2,1)S(1)} %convert_element_type.84), channel_id=1, source_target_pairs={{0,32},{32,64},{64,96},{96,128},{128,160},{160,192},{192,224},{1,3... | collective-permute-start | bytes 9224 | tf_op jit(solution)/shard_map/while/body/eval_jaxpr/ppermute | solution.py:30
  818.8 37.9 %collective-permute-start = (bf16[2,24,64,256]{3,2,1,0:T(8,128)(2,1)}, bf16[2,24,64,256]{3,2,1,0:T(8,128)(2,1)S(1)}, u32[]{:S(2)}, u32[]{:S(2)}) collective-permute-start(bf16[2,24,64,256]{3,2,1,0:T(8,128)(2,1)} %convert_element_type.82), channel_id=1, source_target_pairs={{0,32},{32,64},{64,96},{96,128},{128,160},{160,192},{192,224},{1,3... | collective-permute-start | bytes 4718600 | tf_op jit(solution)/shard_map/while/body/eval_jaxpr/ppermute | solution.py:30
  820.1 36.6 %collective-permute-start.1 = (bf16[24,256]{1,0:T(8,128)(2,1)S(1)}, bf16[24,256]{1,0:T(8,128)(2,1)S(1)}, u32[]{:S(2)}, u32[]{:S(2)}) collective-permute-start(bf16[24,256]{1,0:T(8,128)(2,1)S(1)} %convert_element_type.83), channel_id=1, source_target_pairs={{0,32},{32,64},{64,96},{96,128},{128,160},{160,192},{192,224},{1,3... | collective-permute-start | bytes 36872 | tf_op jit(solution)/shard_map/while/body/eval_jaxpr/ppermute | solution.py:30
  821.5 35.3 %collective-permute-start.2 = (bf16[24,64]{1,0:T(8,128)(2,1)S(1)}, bf16[24,64]{1,0:T(8,128)(2,1)S(1)}, u32[]{:S(2)}, u32[]{:S(2)}) collective-permute-start(bf16[24,64]{1,0:T(8,128)(2,1)S(1)} %convert_element_type.84), channel_id=1, source_target_pairs={{0,32},{32,64},{64,96},{96,128},{128,160},{160,192},{192,224},{1,3... | collective-permute-start | bytes 9224 | tf_op jit(solution)/shard_map/while/body/eval_jaxpr/ppermute | solution.py:30
  861.5 37.2 %collective-permute-start = (bf16[2,24,64,256]{3,2,1,0:T(8,128)(2,1)}, bf16[2,24,64,256]{3,2,1,0:T(8,128)(2,1)S(1)}, u32[]{:S(2)}, u32[]{:S(2)}) collective-permute-start(bf16[2,24,64,256]{3,2,1,0:T(8,128)(2,1)} %convert_element_type.82), channel_id=1, source_target_pairs={{0,32},{32,64},{64,96},{96,128},{128,160},{160,192},{192,224},{1,3... | collective-permute-start | bytes 4718600 | tf_op jit(solution)/shard_map/while/body/eval_jaxpr/ppermute | solution.py:30
  862.8 35.9 %collective-permute-start.1 = (bf16[24,256]{1,0:T(8,128)(2,1)S(1)}, bf16[24,256]{1,0:T(8,128)(2,1)S(1)}, u32[]{:S(2)}, u32[]{:S(2)}) collective-permute-start(bf16[24,256]{1,0:T(8,128)(2,1)S(1)} %convert_element_type.83), channel_id=1, source_target_pairs={{0,32},{32,64},{64,96},{96,128},{128,160},{160,192},{192,224},{1,3... | collective-permute-start | bytes 36872 | tf_op jit(solution)/shard_map/while/body/eval_jaxpr/ppermute | solution.py:30
  864.1 34.6 %collective-permute-start.2 = (bf16[24,64]{1,0:T(8,128)(2,1)S(1)}, bf16[24,64]{1,0:T(8,128)(2,1)S(1)}, u32[]{:S(2)}, u32[]{:S(2)}) collective-permute-start(bf16[24,64]{1,0:T(8,128)(2,1)S(1)} %convert_element_type.84), channel_id=1, source_target_pairs={{0,32},{32,64},{64,96},{96,128},{128,160},{160,192},{192,224},{1,3... | collective-permute-start | bytes 9224 | tf_op jit(solution)/shard_map/while/body/eval_jaxpr/ppermute | solution.py:30
  903.3 36.2 %collective-permute-start = (bf16[2,24,64,256]{3,2,1,0:T(8,128)(2,1)}, bf16[2,24,64,256]{3,2,1,0:T(8,128)(2,1)S(1)}, u32[]{:S(2)}, u32[]{:S(2)}) collective-permute-start(bf16[2,24,64,256]{3,2,1,0:T(8,128)(2,1)} %convert_element_type.82), channel_id=1, source_target_pairs={{0,32},{32,64},{64,96},{96,128},{128,160},{160,192},{192,224},{1,3... | collective-permute-start | bytes 4718600 | tf_op jit(solution)/shard_map/while/body/eval_jaxpr/ppermute | solution.py:30
  904.6 34.9 %collective-permute-start.1 = (bf16[24,256]{1,0:T(8,128)(2,1)S(1)}, bf16[24,256]{1,0:T(8,128)(2,1)S(1)}, u32[]{:S(2)}, u32[]{:S(2)}) collective-permute-start(bf16[24,256]{1,0:T(8,128)(2,1)S(1)} %convert_element_type.83), channel_id=1, source_target_pairs={{0,32},{32,64},{64,96},{96,128},{128,160},{160,192},{192,224},{1,3... | collective-permute-start | bytes 36872 | tf_op jit(solution)/shard_map/while/body/eval_jaxpr/ppermute | solution.py:30
  944.3 800.1 %collective-permute-start = (bf16[2,24,64,256]{3,2,1,0:T(8,128)(2,1)}, bf16[2,24,64,256]{3,2,1,0:T(8,128)(2,1)S(1)}, u32[]{:S(2)}, u32[]{:S(2)}) collective-permute-start(bf16[2,24,64,256]{3,2,1,0:T(8,128)(2,1)} %convert_element_type.82), channel_id=1, source_target_pairs={{0,32},{32,64},{64,96},{96,128},{128,160},{160,192},{192,224},{1,3... | collective-permute-start | bytes 4718600 | tf_op jit(solution)/shard_map/while/body/eval_jaxpr/ppermute | solution.py:30
  945.6 798.8 %collective-permute-start.1 = (bf16[24,256]{1,0:T(8,128)(2,1)S(1)}, bf16[24,256]{1,0:T(8,128)(2,1)S(1)}, u32[]{:S(2)}, u32[]{:S(2)}) collective-permute-start(bf16[24,256]{1,0:T(8,128)(2,1)S(1)} %convert_element_type.83), channel_id=1, source_target_pairs={{0,32},{32,64},{64,96},{96,128},{128,160},{160,192},{192,224},{1,3... | collective-permute-start | bytes 36872 | tf_op jit(solution)/shard_map/while/body/eval_jaxpr/ppermute | solution.py:30
  946.9 797.5 %collective-permute-start.2 = (bf16[24,64]{1,0:T(8,128)(2,1)S(1)}, bf16[24,64]{1,0:T(8,128)(2,1)S(1)}, u32[]{:S(2)}, u32[]{:S(2)}) collective-permute-start(bf16[24,64]{1,0:T(8,128)(2,1)S(1)} %convert_element_type.84), channel_id=1, source_target_pairs={{0,32},{32,64},{64,96},{96,128},{128,160},{160,192},{192,224},{1,3... | collective-permute-start | bytes 9224 | tf_op jit(solution)/shard_map/while/body/eval_jaxpr/ppermute | solution.py:30
  1859.5 36.1 %collective-permute-start = (bf16[2,24,64,256]{3,2,1,0:T(8,128)(2,1)}, bf16[2,24,64,256]{3,2,1,0:T(8,128)(2,1)S(1)}, u32[]{:S(2)}, u32[]{:S(2)}) collective-permute-start(bf16[2,24,64,256]{3,2,1,0:T(8,128)(2,1)} %convert_element_type.82), channel_id=1, source_target_pairs={{0,32},{32,64},{64,96},{96,128},{128,160},{160,192},{192,224},{1,3... | collective-permute-start | bytes 4718600 | tf_op jit(solution)/shard_map/while/body/eval_jaxpr/ppermute | solution.py:30
  1860.8 34.8 %collective-permute-start.1 = (bf16[24,256]{1,0:T(8,128)(2,1)S(1)}, bf16[24,256]{1,0:T(8,128)(2,1)S(1)}, u32[]{:S(2)}, u32[]{:S(2)}) collective-permute-start(bf16[24,256]{1,0:T(8,128)(2,1)S(1)} %convert_element_type.83), channel_id=1, source_target_pairs={{0,32},{32,64},{64,96},{96,128},{128,160},{160,192},{192,224},{1,3... | collective-permute-start | bytes 36872 | tf_op jit(solution)/shard_map/while/body/eval_jaxpr/ppermute | solution.py:30
  2010.7 34.6 %collective-permute-start = (bf16[2,24,64,256]{3,2,1,0:T(8,128)(2,1)}, bf16[2,24,64,256]{3,2,1,0:T(8,128)(2,1)S(1)}, u32[]{:S(2)}, u32[]{:S(2)}) collective-permute-start(bf16[2,24,64,256]{3,2,1,0:T(8,128)(2,1)} %convert_element_type.82), channel_id=1, source_target_pairs={{0,32},{32,64},{64,96},{96,128},{128,160},{160,192},{192,224},{1,3... | collective-permute-start | bytes 4718600 | tf_op jit(solution)/shard_map/while/body/eval_jaxpr/ppermute | solution.py:30
  (52 other events, 284.6 us)
